TPU v7x, 32 devices: a whole 2x2x4 slice. The times are simulated.
32 devices in a mesh: groups: 2 (over y), blk: 4 (over z), tok: 4 (over x, core).
Axes of the slice: x: 2, y: 2, z: 4, core: 2. Of those that a mesh axis runs over, the one named last changes fastest.
Arguments:
- inputs: bfloat16 [12288, 2048], P(('groups', 'tok'), 'blk'), parts along dimension 0, may hold values from -6 to 6
- targets: bfloat16 [12288, 2048], P(('groups', 'tok'), 'blk'), parts along dimension 0, may hold values from -6 to 6
- left_factor: bfloat16 [16, 256, 256], P(('groups', 'blk')), parts along dimension 0, may hold values from -0.375 to 0.375
- right_factor: bfloat16 [16, 256, 256], P(('groups', 'blk')), parts along dimension 0, may hold values from -0.375 to 0.375
Outputs:
- grad_left: float32 [16, 256, 256], P(('groups', 'blk'), 'tok'), parts along dimension 0
- grad_right: float32 [16, 256, 256], P(('groups', 'blk'), 'tok'), parts along dimension 0
There are 2 independent parts, one for each index of `groups`. A program takes and returns all parts, laid end to end along the dimension named above; each array names one. Nothing has to cross between parts.
All inputs are finite; a program needn't handle non-finite values.
Results may differ from a plain program's by a relative error of at most 0.0015.
Values may be sent and summed in bfloat16 or wider, within the bound.
No kernel may reach another device: no remote copies, remote signals or barrier semaphores. Data moves between devices by JAX's collectives and lax.ppermute only.
A program may use at most 64 MiB of HBM per device.

v0:
```python
import jax
import jax.numpy as jnp
from jax import lax
from jax.sharding import PartitionSpec as P


def on_device(inputs, targets, left_factor, right_factor):
    local_blocks = left_factor.shape[0]
    block_width = left_factor.shape[1]
    tok_rows = inputs.shape[0]
    peer_count = lax.axis_size("blk")
    all_blocks = local_blocks * peer_count
    stride_len = block_width // all_blocks
    shaped = inputs.reshape(tok_rows, local_blocks, block_width)
    first_out = jnp.einsum(
        "tki,kji->kjt", shaped, left_factor, preferred_element_type=jnp.float32
    ).astype(jnp.bfloat16)
    outgoing = first_out.reshape(local_blocks, peer_count, local_blocks, stride_len, tok_rows)
    right_view = right_factor.reshape(local_blocks, block_width, all_blocks, stride_len)
    arrived = lax.all_to_all(outgoing, "blk", split_axis=1, concat_axis=0, tiled=True)
    mixed_part = arrived[:, 0]
    student_part = jnp.einsum(
        "gokm,kgmt->got", right_view, mixed_part, preferred_element_type=jnp.float32
    )
    student_four = student_part[:, :, None, :]
    student = student_four[:, :, 0, :]
    truth = targets.reshape(tok_rows, local_blocks, block_width).transpose(1, 2, 0)
    error_rows = (student - truth.astype(jnp.float32)).astype(jnp.bfloat16)
    inverse_rows = jnp.float32(1.0 / tok_rows)
    term_right = jnp.einsum(
        "got,kgmt->gokm", error_rows, mixed_part, preferred_element_type=jnp.float32
    ).reshape(local_blocks, block_width, block_width)
    backward_in = jnp.einsum(
        "gokm,got->kgmt", right_view, error_rows, preferred_element_type=jnp.float32
    ).astype(jnp.bfloat16)
    returned = lax.all_to_all(backward_in, "blk", split_axis=0, concat_axis=1, tiled=True)
    back_first = returned.reshape(local_blocks, block_width, tok_rows)
    term_left = jnp.einsum("kjt,tki->kji", back_first, shaped, preferred_element_type=jnp.float32)
    summed_left, summed_right = (
        lax.psum_scatter(term_left, "tok", scatter_dimension=1, tiled=True),
        lax.psum_scatter(term_right, "tok", scatter_dimension=1, tiled=True),
    )
    return (summed_left * inverse_rows, summed_right * inverse_rows)


def solution(mesh):
    in_specs = (
        P(("groups", "tok"), "blk"),
        P(("groups", "tok"), "blk"),
        P(("groups", "blk"), None, None),
        P(("groups", "blk"), None, None),
    )
    out_specs = (P(("groups", "blk"), "tok", None), P(("groups", "blk"), "tok", None))
    return jax.shard_map(
        on_device, mesh=mesh, in_specs=in_specs, out_specs=out_specs, check_vma=False
    )
```

profile of v0, /device:TPU:0, one launch (start us, length us, event | category | flops | bytes accessed | tf_op | source)
XLA Modules:
  0.0 133.3 jit_solution(9672742158649602140)
XLA Ops:
  7.2 0.0 copy-start
  7.2 0.9 copy-done
  8.1 2.0 %convolution_convert_fusion = bf16[2,256,1536]{2,1,0:T(8,128)(2,1)S(1)} fusion(bf16[2,256,256]{2,1,0:T(8,128)(2,1)S(1)} %copy-done, bf16[192,2,8,256]{3,2,1,0:T(8,128)(2,1)} %bitcast.57), kind=kOutput, calls=%fused_computation.3 | convolution fusion | flops 403439616 | bytes 3407872 | tf_op jit(solution)/shard_map/tki,kji->kjt/dot_general | solution.py:15
  10.1 1.3 copy.26
  11.4 0.0 copy-start.4
  11.4 6.5 %all-to-all-start = ((bf16[2,4,2,32,1536]{4,3,2,0,1:T(8,128)(2,1)}), bf16[2,4,2,32,1536]{4,3,2,0,1:T(8,128)(2,1)S(1)}, u32[]{:S(2)}, u32[]{:S(2)}) async-start(bf16[2,4,2,32,1536]{4,3,2,0,1:T(8,128)(2,1)} %copy.26), calls=%async_computation | async-start | bytes 3145728 | tf_op jit(solution)/shard_map/all_to_all | solution.py:20
  17.9 0.0 copy-done.4
  17.9 0.8 copy.28
  18.7 1.7 %copy.29 = bf16[1536,512]{0,1:T(8,128)(2,1)S(1)} copy(bf16[1536,512]{1,0:T(8,128)(2,1)} %param.5) | data formatting | bytes 3145728 | tf_op args[1]
  20.4 2.0 %copy.30 = f32[1536,2,256]{2,0,1:T(8,128)} copy(bf16[1536,2,256]{0,2,1:T(8,128)(2,1)S(1)} %bitcast.53) | data formatting | bytes 4718592 | tf_op jit(solution)/shard_map/convert_element_type | solution.py:28
  22.5 32.4 %all-to-all-done = bf16[2,4,2,32,1536]{4,3,2,0,1:T(8,128)(2,1)S(1)} async-done(((bf16[2,4,2,32,1536]{4,3,2,0,1:T(8,128)(2,1)}), bf16[2,4,2,32,1536]{4,3,2,0,1:T(8,128)(2,1)S(1)}, u32[]{:S(2)}, u32[]{:S(2)}) %all-to-all-start) | async-done | bytes 1572896 | tf_op jit(solution)/shard_map/all_to_all | solution.py:20
  54.8 0.0 copy-start.1
  54.8 0.1 copy.27
  54.9 0.0 copy-start.2
  55.0 2.3 %copy-done.1 = f32[1536,2,256]{2,0,1:T(8,128)S(1)} copy-done((f32[1536,2,256]{2,0,1:T(8,128)S(1)}, f32[1536,2,256]{2,0,1:T(8,128)}, u32[]{:S(2)}) %copy-start.1) | copy-done | bytes 3145752
  57.3 0.0 copy-start.5
  57.3 1.8 %fusion.1 = bf16[2,256,1536]{1,2,0:T(8,128)(2,1)S(1)} fusion(f32[1536,2,256]{2,0,1:T(8,128)S(1)} %copy-done.1, bf16[8,2,32,1536]{3,2,0,1:T(8,128)(2,1)S(1)} %bitcast.54, bf16[2,256,8,32]{1,3,2,0:T(8,128)(2,1)} %bitcast.60), kind=kOutput, calls=%fused_computation.2 | convolution fusion | flops 404226048 | bytes 6553600 | tf_op jit(solution)/shard_map/gokm,kgmt->got/dot_general | solution.py:22
  59.1 0.0 copy-done.2
  59.1 0.0 copy-done.5
  59.1 0.6 fusion.9
  59.7 0.2 convert_bitcast_fusion
  59.9 1.3 copy.32
  61.2 3.6 %all-to-all-start.1 = ((bf16[8,2,32,1536]{3,2,1,0:T(8,128)(2,1)}), bf16[8,2,32,1536]{3,2,1,0:T(8,128)(2,1)S(1)}, u32[]{:S(2)}, u32[]{:S(2)}) async-start(bf16[8,2,32,1536]{3,2,1,0:T(8,128)(2,1)} %copy.32), calls=%async_computation.1 | async-start | bytes 3145728 | tf_op jit(solution)/shard_map/all_to_all | solution.py:36
  64.8 0.0 reduce-scatter.5.cloned.1.call-start
  64.8 2.8 %fusion.5 = f32[2,256,8,32]{1,3,2,0:T(8,128)} fusion(bf16[8,2,32,1536]{3,2,0,1:T(8,128)(2,1)} %bitcast.55, bf16[2,256,1536]{1,2,0:T(8,128)(2,1)S(1)} %fusion.1), kind=kOutput, calls=%fused_computation.7 | convolution fusion | flops 402653184 | bytes 3670016 | tf_op jit(solution)/shard_map/got,kgmt->gokm/dot_general | solution.py:30
  67.6 2.0 %copy.36 = f32[2,256,256]{2,1,0:T(8,128)} copy(f32[2,256,256]{1,2,0:T(8,128)} %bitcast.59) | data formatting | bytes 1048576 | tf_op jit(solution)/shard_map/reshape | solution.py:32
  69.6 0.0 reduce-scatter.5.cloned.1.call-update
  69.7 0.0 reduce-scatter.3.cloned.1.call-start
  69.7 31.5 %all-to-all-done.1 = bf16[8,2,32,1536]{3,2,1,0:T(8,128)(2,1)S(1)} async-done(((bf16[8,2,32,1536]{3,2,1,0:T(8,128)(2,1)}), bf16[8,2,32,1536]{3,2,1,0:T(8,128)(2,1)S(1)}, u32[]{:S(2)}, u32[]{:S(2)}) %all-to-all-start.1) | async-done | bytes 1572896 | tf_op jit(solution)/shard_map/all_to_all | solution.py:36
  101.2 0.0 copy-start.3
  101.2 0.1 copy.33
  101.3 1.3 copy-done.3
  102.6 1.4 %fusion.2 = f32[2,256,256]{2,1,0:T(8,128)} fusion(bf16[2,256,1536]{2,1,0:T(8,128)(2,1)S(1)} %bitcast.56, bf16[192,2,8,256]{3,2,1,0:T(8,128)(2,1)S(1)} %bitcast.58), kind=kOutput, calls=%fused_computation.4 | convolution fusion | flops 402653184 | bytes 3670016 | tf_op jit(solution)/shard_map/kjt,tki->kji/dot_general | solution.py:38
  104.0 0.0 reduce-scatter.3.cloned.1.call-update
  104.0 0.0 reduce-scatter.5.cloned.1.call-done
  104.0 1.6 %broadcast_multiply_fusion = f32[2,64,256]{2,1,0:T(8,128)} fusion(f32[2,64,256]{2,1,0:T(8,128)} %reduce-scatter.5.cloned.1.call-done), kind=kLoop, calls=%fused_computation.12 | loop fusion | flops 32768 | bytes 262144 | tf_op jit(solution)/shard_map/mul | solution.py:43
  105.6 19.3 %reduce-scatter.3.cloned.1.call-done = f32[2,64,256]{2,1,0:T(8,128)} async-done(((f32[2,256,256]{2,1,0:T(8,128)}), f32[2,64,256]{2,1,0:T(8,128)}) %reduce-scatter.3.cloned.1.call-update) | async-done | bytes 131088 | tf_op jit(solution)/shard_map/reduce_scatter | solution.py:40
  124.9 1.6 %broadcast_multiply_fusion.1 = f32[2,64,256]{2,1,0:T(8,128)} fusion(f32[2,64,256]{2,1,0:T(8,128)} %reduce-scatter.3.cloned.1.call-done), kind=kLoop, calls=%fused_computation.13 | loop fusion | flops 32768 | bytes 262144 | tf_op jit(solution)/shard_map/mul | solution.py:43
Async XLA Ops:
  7.2 1.0 copy-start
  11.4 6.5 %copy-start.4 = (bf16[2,256,256]{2,1,0:T(8,128)(2,1)S(1)}, bf16[2,256,256]{2,1,0:T(8,128)(2,1)}, u32[]{:S(2)}) copy-start(bf16[2,256,256]{2,1,0:T(8,128)(2,1)} %param.7) | copy-start | bytes 786436
  11.4 43.4 %all-to-all-start = ((bf16[2,4,2,32,1536]{4,3,2,0,1:T(8,128)(2,1)}), bf16[2,4,2,32,1536]{4,3,2,0,1:T(8,128)(2,1)S(1)}, u32[]{:S(2)}, u32[]{:S(2)}) async-start(bf16[2,4,2,32,1536]{4,3,2,0,1:T(8,128)(2,1)} %copy.26), calls=%async_computation | async-start | bytes 3145728 | tf_op jit(solution)/shard_map/all_to_all | solution.py:20
  54.8 2.5 %copy-start.1 = (f32[1536,2,256]{2,0,1:T(8,128)S(1)}, f32[1536,2,256]{2,0,1:T(8,128)}, u32[]{:S(2)}) copy-start(f32[1536,2,256]{2,0,1:T(8,128)} %copy.30) | copy-start | bytes 9437188
  54.9 4.1 %copy-start.2 = (bf16[4,2,1,2,32,1536]{5,4,1,0,3,2:T(8,128)(2,1)}, bf16[4,2,1,2,32,1536]{5,4,1,0,3,2:T(8,128)(2,1)S(1)}, u32[]{:S(2)}) copy-start(bf16[4,2,1,2,32,1536]{5,4,1,0,3,2:T(8,128)(2,1)S(1)} %copy.27) | copy-start | bytes 4718596
  57.3 1.8 %copy-start.5 = (bf16[2,256,256]{2,1,0:T(8,128)(2,1)S(1)}, bf16[2,256,256]{2,1,0:T(8,128)(2,1)}, u32[]{:S(2)}) copy-start(bf16[2,256,256]{2,1,0:T(8,128)(2,1)} %param.7) | copy-start | bytes 786436
  61.2 40.0 %all-to-all-start.1 = ((bf16[8,2,32,1536]{3,2,1,0:T(8,128)(2,1)}), bf16[8,2,32,1536]{3,2,1,0:T(8,128)(2,1)S(1)}, u32[]{:S(2)}, u32[]{:S(2)}) async-start(bf16[8,2,32,1536]{3,2,1,0:T(8,128)(2,1)} %copy.32), calls=%async_computation.1 | async-start | bytes 3145728 | tf_op jit(solution)/shard_map/all_to_all | solution.py:36
  64.8 39.3 %reduce-scatter.5.cloned.1.call-start = ((), (), s32[]{:S(2)}) async-start(), calls=%async_computation.5 | async-start | bytes 655360 | tf_op jit(solution)/shard_map/reduce_scatter | solution.py:41
  69.7 55.3 %reduce-scatter.3.cloned.1.call-start = ((), (), s32[]{:S(2)}) async-start(), calls=%async_computation.4 | async-start | bytes 655360 | tf_op jit(solution)/shard_map/reduce_scatter | solution.py:40
  101.2 1.4 %copy-start.3 = (bf16[1536,512]{1,0:T(8,128)(2,1)S(1)}, bf16[1536,512]{1,0:T(8,128)(2,1)}, u32[]{:S(2)}) copy-start(bf16[1536,512]{1,0:T(8,128)(2,1)} %param.4) | copy-start | bytes 4718596
Sparse Core Ops, SparseCore 0:
  69.8 23.0 reduce-scatter.4
  104.1 20.7 reduce-scatter.2
where the time goes:
time: 134 us; the launch traced here: 133 us
  waiting for transfers between devices  83.2 us (62%)
  between operations  14.1 us (11%)
  local copies, waits for them, and re-layouts  14 us (10%)
  starting transfers between devices  10.1 us (8%)
  matrix products  8.54 us (6%)
  other arithmetic  3.34 us (2%)
    all_to_all x1, waiting for transfers between devices, on_device(): lax.all_to_all(outgoing, 'blk', split_axis=1, concat_axis=0, tiled=True)  32.4 us
    all_to_all x1, waiting for transfers between devices, on_device(): lax.all_to_all(backward_in, 'blk', split_axis=0, concat_axis=1, tiled=True)  31.5 us
    reduce_scatter x1, waiting for transfers between devices, on_device(): lax.psum_scatter(term_left, 'tok', scatter_dimension=1, tiled=True)  19.3 us
    unnamed x14, local copies, waits for them, and re-layouts  7.16 us
    all_to_all x1, starting transfers between devices, on_device(): lax.all_to_all(outgoing, 'blk', split_axis=1, concat_axis=0, tiled=True)  6.45 us
    all_to_all x1, starting transfers between devices, on_device(): lax.all_to_all(backward_in, 'blk', split_axis=0, concat_axis=1, tiled=True)  3.56 us
    mul x2, other arithmetic, on_device(): return (summed_left * inverse_rows, summed_right * inverse_rows)  3.14 us
    dot_general x1, matrix products, on_device(): jnp.einsum('got,kgmt->gokm', error_rows, mixed_part, preferred_element_ty...  2.79 us
  transfers between devices with their start and end apart: 4, of which 3 were waited for; matrix products, arithmetic and copies ran while one was open for 9% of the time, Pallas kernels for 0%

commit v1 on v0

--- a/solution.py
+++ b/solution.py
@@ -17,7 +17,19 @@
     ).astype(jnp.bfloat16)
     outgoing = first_out.reshape(local_blocks, peer_count, local_blocks, stride_len, tok_rows)
     right_view = right_factor.reshape(local_blocks, block_width, all_blocks, stride_len)
-    arrived = lax.all_to_all(outgoing, "blk", split_axis=1, concat_axis=0, tiled=True)
+    ways, here = (lax.axis_size("blk"), lax.axis_index("blk"))
+    width = outgoing.shape[1] // ways
+    shape = list(outgoing.shape)
+    shape[1] = width
+    height = shape[0]
+    shape[0] = height * ways
+    full = jnp.zeros(shape, outgoing.dtype)
+    for mask in range(ways):
+        part = lax.dynamic_slice_in_dim(outgoing, (here ^ mask) * width, width, axis=1)
+        if mask:
+            part = lax.ppermute(part, "blk", [(d, d ^ mask) for d in range(ways)])
+        full = lax.dynamic_update_slice_in_dim(full, part, (here ^ mask) * height, axis=0)
+    arrived = full
     mixed_part = arrived[:, 0]
     student_part = jnp.einsum(
         "gokm,kgmt->got", right_view, mixed_part, preferred_element_type=jnp.float32

time: 134 us -> 128 us (0.955)
  waiting for transfers between devices: 83.2 us -> 72.2 us
  starting transfers between devices: 10.1 us -> 14.5 us
  local copies, waits for them, and re-layouts: 14 us -> 16.1 us
    all_to_all x1 -> x0, waiting for transfers between devices: 32.4 us -> none  [on_device(): lax.all_to_all(outgoing, 'blk', split_axis=1, concat_axis=0, tiled=True)]
    ppermute x0 -> x3, waiting for transfers between devices: none -> 21.9 us  [on_device(): part = lax.ppermute(part, 'blk', [(d, d ^ mask) for d in range(ways)])]
    all_to_all x1 -> x0, starting transfers between devices: 6.45 us -> none  [on_device(): lax.all_to_all(outgoing, 'blk', split_axis=1, concat_axis=0, tiled=True)]
    ppermute x0 -> x3, starting transfers between devices: none -> 5.62 us  [on_device(): part = lax.ppermute(part, 'blk', [(d, d ^ mask) for d in range(ways)])]
    all_to_all x1, starting transfers between devices: 3.56 us -> 8.8 us  [on_device(): lax.all_to_all(backward_in, 'blk', split_axis=0, concat_axis=1, tiled=True)]
    dynamic_update_slice x0 -> x4, local copies, waits for them, and re-layouts: none -> 3.1 us  [on_device(): lax.dynamic_update_slice_in_dim(full, part, (here ^ mask) * height, axis=0)]
    unnamed x14 -> x19, local copies, waits for them, and re-layouts: 7.16 us -> 6.46 us
  transfers between devices with their start and end apart: 4 -> 6, of which waited for: 3 -> 4; matrix products, arithmetic and copies ran while one was open for 9% -> 11% of each run, Pallas kernels for 0% -> 0%
where the time goes in v1:
time: 128 us
  waiting for transfers between devices  72.2 us (56%)
  local copies, waits for them, and re-layouts  16.1 us (13%)
  starting transfers between devices  14.5 us (11%)
  between operations  14.2 us (11%)
  matrix products  7.53 us (6%)
  other arithmetic  3.34 us (3%)
    all_to_all x1, waiting for transfers between devices, on_device(): lax.all_to_all(backward_in, 'blk', split_axis=0, concat_axis=1, tiled=True)  30.9 us
    ppermute x3, waiting for transfers between devices, on_device(): part = lax.ppermute(part, 'blk', [(d, d ^ mask) for d in range(ways)])  21.9 us
    reduce_scatter x1, waiting for transfers between devices, on_device(): lax.psum_scatter(term_left, 'tok', scatter_dimension=1, tiled=True)  19.3 us
    all_to_all x1, starting transfers between devices, on_device(): lax.all_to_all(backward_in, 'blk', split_axis=0, concat_axis=1, tiled=True)  8.8 us
    unnamed x19, local copies, waits for them, and re-layouts  6.46 us
    ppermute x3, starting transfers between devices, on_device(): part = lax.ppermute(part, 'blk', [(d, d ^ mask) for d in range(ways)])  5.62 us
    mul x2, other arithmetic, on_device(): return (summed_left * inverse_rows, summed_right * inverse_rows)  3.14 us
    dynamic_update_slice x4, local copies, waits for them, and re-layouts, on_device(): lax.dynamic_update_slice_in_dim(full, part, (here ^ mask) * height, axis=0)  3.1 us
  transfers between devices with their start and end apart: 6, of which 4 were waited for; matrix products, arithmetic and copies ran while one was open for 11% of the time, Pallas kernels for 0%

profile of v1, /device:TPU:0, one launch (start us, length us, event | category | flops | bytes accessed | tf_op | source)
XLA Modules:
  0.0 127.8 jit_solution(15357030064259505837)
XLA Ops:
  7.2 0.0 copy-start
  7.2 0.9 copy-done
  8.1 2.0 %convolution_convert_fusion = bf16[2,256,1536]{2,1,0:T(8,128)(2,1)S(1)} fusion(bf16[2,256,256]{2,1,0:T(8,128)(2,1)S(1)} %copy-done, bf16[192,2,8,256]{3,2,1,0:T(8,128)(2,1)} %bitcast.58), kind=kOutput, calls=%fused_computation.3 | convolution fusion | flops 403439616 | bytes 3407872 | tf_op jit(solution)/shard_map/tki,kji->kjt/dot_general | solution.py:15
  10.1 0.9 constant_dynamic-slice_fusion
  11.0 0.0 copy-start.2
  11.0 0.8 copy.50
  11.8 3.0 %collective-permute-start = (bf16[2,1,2,32,1536]{4,3,0,2,1:T(8,128)(2,1)}, bf16[2,1,2,32,1536]{4,3,0,2,1:T(8,128)(2,1)}, u32[]{:S(2)}, u32[]{:S(2)}) collective-permute-start(bf16[2,1,2,32,1536]{4,3,0,2,1:T(8,128)(2,1)} %copy.50), channel_id=1, source_target_pairs={{0,4},{4,0},{8,12},{12,8},{1,5},{5,1},{9,13},{13,9},{2,6},{6,2},{1... | collective-permute-start | bytes 1179656 | tf_op jit(solution)/shard_map/ppermute | solution.py:30
  14.8 0.8 copy.51
  15.6 2.6 %collective-permute-start.1 = (bf16[2,1,2,32,1536]{4,3,0,2,1:T(8,128)(2,1)}, bf16[2,1,2,32,1536]{4,3,0,2,1:T(8,128)(2,1)}, u32[]{:S(2)}, u32[]{:S(2)}) collective-permute-start(bf16[2,1,2,32,1536]{4,3,0,2,1:T(8,128)(2,1)} %copy.51), channel_id=1, source_target_pairs={{0,8},{4,12},{8,0},{12,4},{1,9},{5,13},{9,1},{13,5},{2,10},{6,14},... | collective-permute-start | bytes 1179656 | tf_op jit(solution)/shard_map/ppermute | solution.py:30
  18.2 0.8 copy.52
  19.0 0.0 collective-permute-start.2
  19.0 0.0 copy-done.2
  19.0 0.7 copy.37
  19.7 0.0 copy-start.6
  19.7 2.0 %copy.38 = f32[1536,2,256]{2,0,1:T(8,128)} copy(bf16[1536,2,256]{0,2,1:T(8,128)(2,1)S(1)} %bitcast.55) | data formatting | bytes 4718592 | tf_op jit(solution)/shard_map/convert_element_type | solution.py:40
  21.7 0.0 copy-done.6
  21.7 0.0 copy-start.5
  21.7 0.1 copy.36
  21.9 0.1 squeeze.11
  22.0 0.7 copy-done.5
  22.7 0.0 copy-start.1
  22.8 8.8 %collective-permute-done = bf16[2,1,2,32,1536]{4,3,0,2,1:T(8,128)(2,1)} collective-permute-done((bf16[2,1,2,32,1536]{4,3,0,2,1:T(8,128)(2,1)}, bf16[2,1,2,32,1536]{4,3,0,2,1:T(8,128)(2,1)}, u32[]{:S(2)}, u32[]{:S(2)}) %collective-permute-start) | collective-permute-done | bytes 393248 | tf_op jit(solution)/shard_map/ppermute | solution.py:30
  31.5 1.0 bitcast_dynamic-update-slice_fusion.2
  32.6 13.1 %collective-permute-done.1 = bf16[2,1,2,32,1536]{4,3,0,2,1:T(8,128)(2,1)} collective-permute-done((bf16[2,1,2,32,1536]{4,3,0,2,1:T(8,128)(2,1)}, bf16[2,1,2,32,1536]{4,3,0,2,1:T(8,128)(2,1)}, u32[]{:S(2)}, u32[]{:S(2)}) %collective-permute-start.1) | collective-permute-done | bytes 393248 | tf_op jit(solution)/shard_map/ppermute | solution.py:30
  45.7 1.0 bitcast_dynamic-update-slice_fusion.1
  46.7 0.0 collective-permute-done.2
  46.7 1.0 bitcast_dynamic-update-slice_fusion
  47.8 0.0 copy-start.3
  47.8 0.0 copy-done.1
  47.8 0.8 fusion.1
  48.6 0.4 copy-done.3
  48.9 0.6 fusion.9
  49.6 0.2 convert_bitcast_fusion
  49.8 1.3 %copy.40 = bf16[8,2,32,1536]{3,2,1,0:T(8,128)(2,1)} copy(bf16[8,2,32,1536]{3,2,0,1:T(8,128)(2,1)S(1)} %convert_bitcast_fusion) | data formatting | bytes 3145728 | tf_op jit(solution)/shard_map/convert_element_type | solution.py:47
  51.1 8.8 %all-to-all-start = ((bf16[8,2,32,1536]{3,2,1,0:T(8,128)(2,1)}), bf16[8,2,32,1536]{3,2,1,0:T(8,128)(2,1)S(1)}, u32[]{:S(2)}, u32[]{:S(2)}) async-start(bf16[8,2,32,1536]{3,2,1,0:T(8,128)(2,1)} %copy.40), calls=%async_computation | async-start | bytes 3145728 | tf_op jit(solution)/shard_map/all_to_all | solution.py:48
  59.9 0.0 reduce-scatter.5.cloned.1.call-start
  59.9 2.8 %fusion.5 = f32[2,256,8,32]{1,3,2,0:T(8,128)} fusion(bf16[8,2,32,1536]{3,2,0,1:T(8,128)(2,1)} %copy-done.3, bf16[2,256,1536]{1,2,0:T(8,128)(2,1)S(1)} %fusion.1), kind=kOutput, calls=%fused_computation.7 | convolution fusion | flops 402653184 | bytes 3670016 | tf_op jit(solution)/shard_map/got,kgmt->gokm/dot_general | solution.py:42
  62.6 2.0 %copy.44 = f32[2,256,256]{2,1,0:T(8,128)} copy(f32[2,256,256]{1,2,0:T(8,128)} %bitcast.60) | data formatting | bytes 1048576 | tf_op jit(solution)/shard_map/reshape | solution.py:44
  64.7 0.0 reduce-scatter.5.cloned.1.call-update
  64.7 0.0 reduce-scatter.3.cloned.1.call-start
  64.8 30.9 %all-to-all-done = bf16[8,2,32,1536]{3,2,1,0:T(8,128)(2,1)S(1)} async-done(((bf16[8,2,32,1536]{3,2,1,0:T(8,128)(2,1)}), bf16[8,2,32,1536]{3,2,1,0:T(8,128)(2,1)S(1)}, u32[]{:S(2)}, u32[]{:S(2)}) %all-to-all-start) | async-done | bytes 1572896 | tf_op jit(solution)/shard_map/all_to_all | solution.py:48
  95.7 0.0 copy-start.4
  95.7 0.1 copy.41
  95.8 1.3 %copy-done.4 = bf16[1536,512]{1,0:T(8,128)(2,1)S(1)} copy-done((bf16[1536,512]{1,0:T(8,128)(2,1)S(1)}, bf16[1536,512]{1,0:T(8,128)(2,1)}, u32[]{:S(2)}) %copy-start.4) | copy-done | bytes 1572888
  97.1 1.4 %fusion.2 = f32[2,256,256]{2,1,0:T(8,128)} fusion(bf16[2,256,1536]{2,1,0:T(8,128)(2,1)S(1)} %bitcast.57, bf16[192,2,8,256]{3,2,1,0:T(8,128)(2,1)S(1)} %bitcast.59), kind=kOutput, calls=%fused_computation.4 | convolution fusion | flops 402653184 | bytes 3670016 | tf_op jit(solution)/shard_map/kjt,tki->kji/dot_general | solution.py:50
  98.5 0.0 reduce-scatter.3.cloned.1.call-update
  98.5 0.0 reduce-scatter.5.cloned.1.call-done
  98.5 1.6 %broadcast_multiply_fusion = f32[2,64,256]{2,1,0:T(8,128)} fusion(f32[2,64,256]{2,1,0:T(8,128)} %reduce-scatter.5.cloned.1.call-done), kind=kLoop, calls=%fused_computation.16 | loop fusion | flops 32768 | bytes 262144 | tf_op jit(solution)/shard_map/mul | solution.py:55
  100.1 19.3 %reduce-scatter.3.cloned.1.call-done = f32[2,64,256]{2,1,0:T(8,128)} async-done(((f32[2,256,256]{2,1,0:T(8,128)}), f32[2,64,256]{2,1,0:T(8,128)}) %reduce-scatter.3.cloned.1.call-update) | async-done | bytes 131088 | tf_op jit(solution)/shard_map/reduce_scatter | solution.py:52
  119.4 1.6 %broadcast_multiply_fusion.1 = f32[2,64,256]{2,1,0:T(8,128)} fusion(f32[2,64,256]{2,1,0:T(8,128)} %reduce-scatter.3.cloned.1.call-done), kind=kLoop, calls=%fused_computation.17 | loop fusion | flops 32768 | bytes 262144 | tf_op jit(solution)/shard_map/mul | solution.py:55
  (1 shorter events, 0.0 us)
Async XLA Ops:
  7.2 1.0 copy-start
  11.0 8.0 %copy-start.2 = (bf16[1536,512]{1,0:T(8,128)(2,1)S(1)}, bf16[1536,512]{1,0:T(8,128)(2,1)}, u32[]{:S(2)}) copy-start(bf16[1536,512]{1,0:T(8,128)(2,1)} %param.5) | copy-start | bytes 4718596
  11.8 19.7 %collective-permute-start = (bf16[2,1,2,32,1536]{4,3,0,2,1:T(8,128)(2,1)}, bf16[2,1,2,32,1536]{4,3,0,2,1:T(8,128)(2,1)}, u32[]{:S(2)}, u32[]{:S(2)}) collective-permute-start(bf16[2,1,2,32,1536]{4,3,0,2,1:T(8,128)(2,1)} %copy.50), channel_id=1, source_target_pairs={{0,4},{4,0},{8,12},{12,8},{1,5},{5,1},{9,13},{13,9},{2,6},{6,2},{1... | collective-permute-start | bytes 1179656 | tf_op jit(solution)/shard_map/ppermute | solution.py:30
  15.6 30.1 %collective-permute-start.1 = (bf16[2,1,2,32,1536]{4,3,0,2,1:T(8,128)(2,1)}, bf16[2,1,2,32,1536]{4,3,0,2,1:T(8,128)(2,1)}, u32[]{:S(2)}, u32[]{:S(2)}) collective-permute-start(bf16[2,1,2,32,1536]{4,3,0,2,1:T(8,128)(2,1)} %copy.51), channel_id=1, source_target_pairs={{0,8},{4,12},{8,0},{12,4},{1,9},{5,13},{9,1},{13,5},{2,10},{6,14},... | collective-permute-start | bytes 1179656 | tf_op jit(solution)/shard_map/ppermute | solution.py:30
  19.0 27.8 %collective-permute-start.2 = (bf16[2,1,2,32,1536]{4,3,0,2,1:T(8,128)(2,1)}, bf16[2,1,2,32,1536]{4,3,0,2,1:T(8,128)(2,1)}, u32[]{:S(2)}, u32[]{:S(2)}) collective-permute-start(bf16[2,1,2,32,1536]{4,3,0,2,1:T(8,128)(2,1)} %copy.52), channel_id=1, source_target_pairs={{0,12},{4,8},{8,4},{12,0},{1,13},{5,9},{9,5},{13,1},{2,14},{6,10},... | collective-permute-start | bytes 1179656 | tf_op jit(solution)/shard_map/ppermute | solution.py:30
  19.7 2.1 %copy-start.6 = (bf16[2,256,256]{2,1,0:T(8,128)(2,1)S(1)}, bf16[2,256,256]{2,1,0:T(8,128)(2,1)}, u32[]{:S(2)}) copy-start(bf16[2,256,256]{2,1,0:T(8,128)(2,1)} %param.7) | copy-start | bytes 786436
  21.7 1.0 copy-start.5
  22.7 25.1 %copy-start.1 = (f32[1536,2,256]{2,0,1:T(8,128)S(1)}, f32[1536,2,256]{2,0,1:T(8,128)}, u32[]{:S(2)}) copy-start(f32[1536,2,256]{2,0,1:T(8,128)} %copy.38) | copy-start | bytes 9437188
  47.8 1.2 copy-start.3
  51.1 44.6 %all-to-all-start = ((bf16[8,2,32,1536]{3,2,1,0:T(8,128)(2,1)}), bf16[8,2,32,1536]{3,2,1,0:T(8,128)(2,1)S(1)}, u32[]{:S(2)}, u32[]{:S(2)}) async-start(bf16[8,2,32,1536]{3,2,1,0:T(8,128)(2,1)} %copy.40), calls=%async_computation | async-start | bytes 3145728 | tf_op jit(solution)/shard_map/all_to_all | solution.py:48
  59.9 38.6 %reduce-scatter.5.cloned.1.call-start = ((), (), s32[]{:S(2)}) async-start(), calls=%async_computation.4 | async-start | bytes 655360 | tf_op jit(solution)/shard_map/reduce_scatter | solution.py:53
  64.7 54.7 %reduce-scatter.3.cloned.1.call-start = ((), (), s32[]{:S(2)}) async-start(), calls=%async_computation.3 | async-start | bytes 655360 | tf_op jit(solution)/shard_map/reduce_scatter | solution.py:52
  95.7 1.4 %copy-start.4 = (bf16[1536,512]{1,0:T(8,128)(2,1)S(1)}, bf16[1536,512]{1,0:T(8,128)(2,1)}, u32[]{:S(2)}) copy-start(bf16[1536,512]{1,0:T(8,128)(2,1)} %param.4) | copy-start | bytes 4718596
Sparse Core Ops, SparseCore 0:
  64.8 23.1 reduce-scatter.4
  98.6 20.7 reduce-scatter.2
